TPU v7x, 128 devices: a whole 4x4x4 slice. The times are simulated.
128 devices in a mesh: gx: 32 (over y, x_hi, z), gy: 4 (over x_lo, core).
Axes of the slice: x: 4 (x_hi: 2, x_lo: 2; x = x_hi * 2 + x_lo), y: 4, z: 4, core: 2. Of those that a mesh axis runs over, the one named last changes fastest.
Arguments:
- density: float32 [512, 128, 512], P('gx', 'gy'), may hold values from -6 to 6
- kernel: bfloat16 [16, 512], replicated, may hold values from -0.125 to 0.125
- electrode: int32 [512], P('gx'), may hold values from 0 to 15
- drift_sign: int32 [8], replicated, may hold values from 0 to 1
Outputs:
- final_density: float32 [512, 128, 512], P('gx', 'gy')
Inputs may be any that keep to these rules, and one draw needn't show every extreme that they name: `electrode`: index into the voltage table. `drift_sign`: 1 makes positive momentum offsets drift toward higher y, 0 toward lower y.
All inputs are finite; a program needn't handle non-finite values.
Results may differ from a plain program's by a relative error of at most 0.024.
Values may be sent and summed in bfloat16 or wider, within the bound.
A program may use at most 192 MiB of HBM per device.

v0:
```python
import functools

import jax
import jax.numpy as jnp
import numpy as np
from jax import lax
from jax.experimental import pallas as pl
from jax.experimental.pallas import tpu as pltpu
from jax.sharding import PartitionSpec as P

NX = 512
NP = 512
XB = 16
YB = 32
NV = 16
PARTS = 128
MESH = pl.DeviceIdType.MESH
F32 = jnp.float32
BF16 = jnp.bfloat16


def shift_kernels():
    k = np.arange(NX)
    kappa = np.where(k > NX // 2, k - NX, k).astype(np.int64)
    n = np.arange(NX)
    rows = np.zeros((8, NX), np.float64)
    for parity in range(2):
        p = parity
        m = (kappa * (NX // 4) * (NP - 1 - 2 * p)) % (NX * NP)
        phase = 2 * np.pi * m / (NX * NP)
        g = np.cos(2 * np.pi * ((n[:, None] * k[None, :]) % NX) / NX - phase[None, :]).sum(1) / NX
        spectrum = np.fft.fft(g)
        g2 = np.fft.ifft(spectrum * spectrum).real
        whole = 127 - p // 2
        whole2 = 255 - p
        rows[parity] = np.roll(g, -whole)[(-n) % NX]
        rows[2 + parity] = np.roll(g2, -whole2)[(-n) % NX]
    return rows.astype(np.float32)


def send_order():
    ring = lambda t: min(t, 4 - t)
    offsets = [o for o in range(64)]
    key = lambda o: -(ring(o // 16) + ring(o // 4 % 4) + ring(o % 4))
    offsets.sort(key=lambda o: (key(o), (o * 37) % 64))
    offsets = offsets[:63]
    packed = []
    for i in range(0, 63, 3):
        trio = offsets[i : i + 3]
        packed.append(trio[0] + 64 * trio[1] + 4096 * trio[2])
    return packed


ORDER = send_order()


def for_each_peer(me, visit):
    y, z, x, core = me

    def group(g, carry):
        code = jnp.int32(0)
        for i, value in enumerate(ORDER):
            code = jnp.where(g == i, jnp.int32(value), code)

        def one(_, code):
            o = lax.rem(code, 64)
            y2 = lax.rem(y + o // 16, 4)
            z2 = lax.rem(z + lax.rem(o // 4, 4), 4)
            x2 = lax.rem(x + lax.rem(o, 4), 4)
            gx = y2 * 8 + (x2 // 2) * 4 + z2
            gy = lax.rem(x2, 2) * 2
            visit(gx, gy)
            visit(gx, gy + 1)
            return code // 64

        lax.fori_loop(0, 3, one, code)
        return carry

    lax.fori_loop(0, len(ORDER), group, 0)
    gx = y * 8 + (x // 2) * 4 + z
    visit(gx, lax.rem(x, 2) * 2 + 1 - core)


def iota(shape, axis):
    return lax.broadcasted_iota(jnp.int32, shape, axis)


def nt_dot(a, b):
    return lax.dot_general(a, b, (((1,), (1,)), ((), ())), preferred_element_type=F32)


def dot(a, b):
    return jnp.dot(a, b, preferred_element_type=F32)


def whole_kernel(
    density,
    kernel,
    electrode,
    drift_sign,
    taps,
    out,
    to_lines,
    lines,
    to_rows,
    rows,
    stage,
    half,
    double,
    drift,
    toeplitz,
    kick,
    offsets,
    send,
    recv,
):
    gx = lax.axis_index("gx")
    gy = lax.axis_index("gy")
    d = gx * 4 + gy
    me = (gx // 8, lax.rem(gx, 4), lax.rem(gx // 4, 2) * 2 + gy // 2, lax.rem(gy, 2))

    barrier = pltpu.get_barrier_semaphore()

    def greet(a, b):
        pl.semaphore_signal(barrier, inc=1, device_id=(a, b), device_id_type=MESH)

    for_each_peer(me, greet)

    def row_tile(ref, a, b):
        return ref.at[pl.ds(pl.multiple_of(a * XB, XB), XB), pl.ds(pl.multiple_of(b * 128, 128), 128)]

    def send_to_lines(r):
        def push(a, b):
            pltpu.make_async_remote_copy(
                src_ref=to_lines.at[a * 4 + b],
                dst_ref=row_tile(lines.at[r], gx, gy),
                send_sem=send.at[2 * r],
                recv_sem=recv.at[2 * r],
                device_id=(a, b),
                device_id_type=MESH,
            ).start()

        for_each_peer(me, push)
        pltpu.make_async_copy(to_lines.at[d], row_tile(lines.at[r], gx, gy), recv.at[2 * r]).start()

    def send_to_rows(r):
        def push(a, b):
            pltpu.make_async_remote_copy(
                src_ref=row_tile(to_rows, a, b),
                dst_ref=rows.at[r, d],
                send_sem=send.at[2 * r + 1],
                recv_sem=recv.at[2 * r + 1],
                device_id=(a, b),
                device_id_type=MESH,
            ).start()

        for_each_peer(me, push)
        pltpu.make_async_copy(row_tile(to_rows, gx, gy), rows.at[r, d], recv.at[2 * r + 1]).start()

    def wait_lines(r):
        pltpu.make_async_copy(lines.at[r], lines.at[r], recv.at[2 * r]).wait()

    def wait_rows(r):
        pltpu.make_async_copy(rows.at[r], rows.at[r], recv.at[2 * r + 1]).wait()

    def wait_sent(s):
        sent = to_lines.at[pl.ds(0, PARTS - 1)]
        pltpu.make_async_copy(sent, sent, send.at[s]).wait()

    eye = (iota((128, 128), 0) == iota((128, 128), 1)).astype(BF16)

    def pack(x, carry):
        block = jnp.concatenate([density[x, :, 128 * j : 128 * j + 128] for j in range(4)], axis=0)
        stage[pl.ds(x, 128, stride=XB), :] = nt_dot(eye, block.astype(BF16))
        return carry

    lax.fori_loop(0, XB, pack, 0)
    to_lines[...] = stage[...].astype(BF16).reshape(PARTS, XB, 128)

    pl.semaphore_wait(barrier, PARTS - 1)
    send_to_lines(0)

    parity = lax.rem(d, 2)

    def circulant(row_even, row_odd, shift):
        row = jnp.where(parity == 0, row_even, row_odd)
        row = pltpu.roll(jnp.broadcast_to(row, (8, NX)), shift, 1)[0:1, :]
        wide = jnp.broadcast_to(row, (NX, NX))
        return pltpu.roll(wide, 0, 1, stride=1, stride_axis=0)

    half[...] = circulant(taps[0:1, :], taps[1:2, :], NX - 127 + d // 2).astype(BF16)
    double[...] = circulant(taps[2:3, :], taps[3:4, :], NX - 255 + d).astype(BF16)

    col = iota((16, 512), 1)
    col_y = (col // 128) * 32 + lax.rem(col, 32)
    col_p = lax.rem(col // 32, 4) * 128 + d
    speed = 0.5 * ((2 * col_p - (NP - 1)).astype(F32) / NP)

    def sign_at(cell):
        slab = cell // 16
        chosen = jnp.zeros((16, 512), jnp.int32)
        for s in range(8):
            chosen = jnp.where(slab == s, drift_sign[s], chosen)
        return (2 * chosen - 1).astype(F32)

    face_low = speed * sign_at(jnp.maximum(col_y - 1, 0))
    face_high = speed * sign_at(col_y)
    keep = 1.0 - jnp.maximum(face_high, 0.0) + jnp.minimum(face_low, 0.0)
    from_next = jnp.where(col_y == 127, 0.0, -jnp.minimum(face_high, 0.0))
    from_prev = jnp.where(col_y == 0, 0.0, jnp.maximum(face_low, 0.0))
    inner = lax.rem(col, 32)
    band = jnp.where(iota((16, 512), 0) == 8, 1.0, 0.0).astype(F32)
    for _ in range(4):
        after = jnp.where(inner == 31, pltpu.roll(band, 512 - 97, 1), pltpu.roll(band, 511, 1))
        before = jnp.where(inner == 0, pltpu.roll(band, 97, 1), pltpu.roll(band, 1, 1))
        band = (
            keep * band
            + from_next * pltpu.roll(after, 1, 0)
            + from_prev * pltpu.roll(before, 15, 0)
        )
    for b in range(4):
        row = iota((128, 512), 0)
        column = iota((128, 512), 1)
        gap = (b * 32 + lax.rem(row, 32)) - ((column // 128) * 32 + lax.rem(column, 32))
        gap = jnp.where(row // 32 == lax.rem(column // 32, 4), gap, 99)
        matrix = jnp.zeros((128, 512), F32)
        for step in range(-4, 5):
            matrix = jnp.where(gap == step, band[8 + step : 9 + step, :], matrix)
        drift[128 * b : 128 * b + 128, :] = matrix.astype(BF16)

    flip = (iota((512, 512), 0) == lax.rem(512 - iota((512, 512), 1), 512)).astype(BF16)
    forward = kernel[...].astype(F32)
    backward = dot(kernel[...], flip)
    ahead = jnp.where(iota((NV, 512), 1) == 0, forward, -forward)
    both = jnp.concatenate([ahead, backward], axis=1)
    for v in range(NV):
        offsets[v] = both[v : v + 1, :]

    lane_block = iota((128, 128), 1) // 32
    wide_block = lax.rem(iota((512, 512), 1) // 32, 4)

    def advect(r, matrix, with_drift, cells):
        if with_drift:
            current = dot(lines[r], drift[...]).astype(BF16)
        else:
            current = lines[r]
        turned = current
        for j in range(1, 4):
            cut = cells * j
            moved = jnp.concatenate([current[cut:], current[:cut]], axis=0)
            turned = jnp.where(wide_block == j, moved, turned)
        to_rows[...] = dot(matrix[...], turned).astype(BF16)

    spread = (
        iota((128, 512), 0) == (iota((128, 512), 1) // 128) * 32 + lax.rem(iota((128, 512), 1), 32)
    ).astype(BF16)

    def build_kicks():
        def build(x, carry):
            base = jnp.broadcast_to(offsets[electrode[x]], (128, 1024))
            base = pltpu.roll(base, 0, 1, stride=1, stride_axis=0).astype(BF16)
            for t in range(4):
                for c in range(4):
                    at = 128 * ((c - t) % 8)
                    toeplitz[128 * t : 128 * t + 128, 128 * c : 128 * c + 128] = base[:, at : at + 128]
            square = dot(toeplitz[...], toeplitz[...])
            kick[x] = (toeplitz[...].astype(F32) + 0.5 * square).astype(BF16)
            return carry

        lax.fori_loop(0, XB, build, 0)

    def kick_rows(r):
        stage[...] = rows[r].reshape(PARTS * XB, 128).astype(F32)

        def one(x, carry):
            current = stage[pl.ds(x, 128, stride=XB), :]
            repeated = dot(current.astype(BF16), spread).astype(BF16)
            operand = jnp.concatenate([repeated[:, 128 * j : 128 * j + 128] for j in range(4)], axis=0)
            product = dot(kick[x], operand)
            change = product[0:128]
            for j in range(1, 4):
                change = jnp.where(lane_block == j, product[128 * j : 128 * j + 128], change)
            stage[pl.ds(x, 128, stride=XB), :] = current + change
            return carry

        lax.fori_loop(0, XB, one, 0)
        wait_sent(2 * r)
        to_lines[...] = stage[...].astype(BF16).reshape(PARTS, XB, 128)

    wait_lines(0)
    advect(0, half, True, 64)
    send_to_rows(0)
    build_kicks()
    wait_rows(0)
    kick_rows(0)
    send_to_lines(1)
    wait_lines(1)
    wait_sent(1)
    advect(1, double, True, 128)
    send_to_rows(1)
    wait_rows(1)
    kick_rows(1)
    send_to_lines(2)
    wait_lines(2)
    wait_sent(3)
    advect(2, half, False, 64)
    send_to_rows(2)
    wait_rows(2)
    stage[...] = rows[2].reshape(PARTS * XB, 128).astype(F32)

    def unpack(x, carry):
        current = stage[pl.ds(x, 128, stride=XB), :].astype(BF16)
        turned = nt_dot(eye, current)
        for j in range(4):
            out[x, :, 128 * j : 128 * j + 128] = turned[32 * j : 32 * j + 32, :]
        return carry

    lax.fori_loop(0, XB, unpack, 0)
    wait_sent(4)
    wait_sent(5)


def on_device(density, kernel, electrode, drift_sign):
    vmem = pl.BlockSpec(memory_space=pltpu.VMEM)
    smem = pl.BlockSpec(memory_space=pltpu.SMEM)
    return pl.pallas_call(
        whole_kernel,
        out_shape=jax.ShapeDtypeStruct(density.shape, F32),
        in_specs=[vmem, vmem, smem, smem, vmem],
        out_specs=vmem,
        scratch_shapes=[
            pltpu.VMEM((PARTS, XB, 128), BF16),
            pltpu.VMEM((3, NX, 512), BF16),
            pltpu.VMEM((NX, 512), BF16),
            pltpu.VMEM((3, PARTS, XB, 128), BF16),
            pltpu.VMEM((PARTS * XB, 128), F32),
            pltpu.VMEM((NX, NX), BF16),
            pltpu.VMEM((NX, NX), BF16),
            pltpu.VMEM((512, 512), BF16),
            pltpu.VMEM((NP, NP), BF16),
            pltpu.VMEM((XB, NP, NP), BF16),
            pltpu.VMEM((NV, 1, 1024), F32),
            pltpu.SemaphoreType.DMA((6,)),
            pltpu.SemaphoreType.DMA((6,)),
        ],
        compiler_params=pltpu.CompilerParams(
            collective_id=0, has_side_effects=True, vmem_limit_bytes=56 << 20
        ),
    )(density, kernel, electrode, drift_sign, jnp.asarray(shift_kernels()))


def solution(mesh):
    return jax.shard_map(
        on_device,
        mesh=mesh,
        in_specs=(P("gx", "gy", None), P(), P("gx"), P()),
        out_specs=P("gx", "gy", None),
        check_vma=False,
    )
```

profile of v0, /device:TPU:0, one launch (start us, length us, event | category | flops | bytes accessed | tf_op | source)
XLA Modules:
  0.0 97.7 jit_solution(8451966741617958405)
XLA Ops:
  0.0 95.4 %shard_map.55 = f32[16,32,512]{2,1,0:T(8,128)} custom-call(f32[16,32,512]{2,1,0:T(8,128)} %density.1, bf16[16,512]{1,0:T(8,128)(2,1)} %kernel.1, s32[16]{0:T(128)} %electrode.1, s32[8]{0:T(128)} %drift_sign.1, f32[8,512]{1,0:T(8,128)} %constant.2.clone.taps), custom_call_target="tpu_custom_call" | custom-call | tf_op jit(solution)/shard_map/pallas_call | solution.py:326
  95.4 2.3 %copy.7 = f32[16,32,512]{2,1,0:T(8,128)} copy(f32[16,32,512]{2,1,0:T(8,128)} %shard_map.55) | data formatting | bytes 2097152
where the time goes:
time: 98.9 us; the launch traced here: 97.7 us
  Pallas kernels  95.4 us (96%)
  local copies, waits for them, and re-layouts  2.29 us (2%)
    pallas_call x1, Pallas kernels, on_device(): pl.pallas_call(whole_kernel, out_shape=jax.ShapeDtypeStruct(density.shape...  95.4 us
    unnamed x1, local copies, waits for them, and re-layouts  2.29 us

commit v1 on v0

--- a/solution.py
+++ b/solution.py
@@ -108,7 +108,7 @@
     half,
     double,
     drift,
-    toeplitz,
+    kicked,
     kick,
     offsets,
     send,
@@ -169,14 +169,38 @@
 
     eye = (iota((128, 128), 0) == iota((128, 128), 1)).astype(BF16)
 
-    def pack(x, carry):
+    for x in range(XB):
         block = jnp.concatenate([density[x, :, 128 * j : 128 * j + 128] for j in range(4)], axis=0)
         stage[pl.ds(x, 128, stride=XB), :] = nt_dot(eye, block.astype(BF16))
-        return carry
-
-    lax.fori_loop(0, XB, pack, 0)
     to_lines[...] = stage[...].astype(BF16).reshape(PARTS, XB, 128)
 
+    flip = (iota((512, 512), 0) == lax.rem(512 - iota((512, 512), 1), 512)).astype(BF16)
+    forward = kernel[...].astype(F32)
+    backward = dot(kernel[...], flip)
+    ahead = jnp.where(iota((NV, 512), 1) == 0, forward, -forward)
+    both = jnp.concatenate([ahead, backward], axis=1)
+    for v in range(NV):
+        offsets[v] = both[v : v + 1, :]
+
+    def build_kicks(start, stop):
+        for x in range(start, stop):
+            base = jnp.broadcast_to(offsets[electrode[x]], (128, 1024))
+            base = pltpu.roll(base, 0, 1, stride=1, stride_axis=0).astype(BF16)
+            shifted = [base[:, 128 * c : 128 * c + 128] for c in range(8)]
+            matrix = jnp.concatenate(
+                [jnp.concatenate([shifted[(c - t) % 8] for c in range(4)], axis=1) for t in range(4)],
+                axis=0,
+            )
+            square = dot(matrix, matrix)
+            for t in range(4):
+                for c in range(4):
+                    at = 128 * ((t - c) % 4)
+                    kick[x, 128 * t : 128 * t + 128, at : at + 128] = (
+                        shifted[(c - t) % 8].astype(F32)
+                        + 0.5 * square[128 * t : 128 * t + 128, 128 * c : 128 * c + 128]
+                    ).astype(BF16)
+
+    build_kicks(0, 4)
     pl.semaphore_wait(barrier, PARTS - 1)
     send_to_lines(0)
 
@@ -228,14 +252,6 @@
             matrix = jnp.where(gap == step, band[8 + step : 9 + step, :], matrix)
         drift[128 * b : 128 * b + 128, :] = matrix.astype(BF16)
 
-    flip = (iota((512, 512), 0) == lax.rem(512 - iota((512, 512), 1), 512)).astype(BF16)
-    forward = kernel[...].astype(F32)
-    backward = dot(kernel[...], flip)
-    ahead = jnp.where(iota((NV, 512), 1) == 0, forward, -forward)
-    both = jnp.concatenate([ahead, backward], axis=1)
-    for v in range(NV):
-        offsets[v] = both[v : v + 1, :]
-
     lane_block = iota((128, 128), 1) // 32
     wide_block = lax.rem(iota((512, 512), 1) // 32, 4)
 
@@ -251,46 +267,29 @@
             turned = jnp.where(wide_block == j, moved, turned)
         to_rows[...] = dot(matrix[...], turned).astype(BF16)
 
-    spread = (
-        iota((128, 512), 0) == (iota((128, 512), 1) // 128) * 32 + lax.rem(iota((128, 512), 1), 32)
-    ).astype(BF16)
-
-    def build_kicks():
-        def build(x, carry):
-            base = jnp.broadcast_to(offsets[electrode[x]], (128, 1024))
-            base = pltpu.roll(base, 0, 1, stride=1, stride_axis=0).astype(BF16)
-            for t in range(4):
-                for c in range(4):
-                    at = 128 * ((c - t) % 8)
-                    toeplitz[128 * t : 128 * t + 128, 128 * c : 128 * c + 128] = base[:, at : at + 128]
-            square = dot(toeplitz[...], toeplitz[...])
-            kick[x] = (toeplitz[...].astype(F32) + 0.5 * square).astype(BF16)
-            return carry
-
-        lax.fori_loop(0, XB, build, 0)
-
     def kick_rows(r):
         stage[...] = rows[r].reshape(PARTS * XB, 128).astype(F32)
-
-        def one(x, carry):
-            current = stage[pl.ds(x, 128, stride=XB), :]
-            repeated = dot(current.astype(BF16), spread).astype(BF16)
-            operand = jnp.concatenate([repeated[:, 128 * j : 128 * j + 128] for j in range(4)], axis=0)
-            product = dot(kick[x], operand)
-            change = product[0:128]
-            for j in range(1, 4):
-                change = jnp.where(lane_block == j, product[128 * j : 128 * j + 128], change)
-            stage[pl.ds(x, 128, stride=XB), :] = current + change
-            return carry
-
-        lax.fori_loop(0, XB, one, 0)
+        for start in range(0, XB, 4):
+            group = range(start, start + 4)
+            current = [stage[pl.ds(x, 128, stride=XB), :] for x in group]
+            operand = [
+                jnp.concatenate([c] + [pltpu.roll(c, 32 * k, 1) for k in range(1, 4)], axis=0).astype(BF16)
+                for c in current
+            ]
+            product = [dot(kick[x], o) for x, o in zip(group, operand)]
+            for x, c, q in zip(group, current, product):
+                change = q[0:128]
+                for j in range(1, 4):
+                    change = jnp.where(lane_block == j, q[128 * j : 128 * j + 128], change)
+                kicked[pl.ds(x, 128, stride=XB), :] = c + change
         wait_sent(2 * r)
-        to_lines[...] = stage[...].astype(BF16).reshape(PARTS, XB, 128)
-
+        to_lines[...] = kicked[...].astype(BF16).reshape(PARTS, XB, 128)
+
+    build_kicks(4, 10)
     wait_lines(0)
     advect(0, half, True, 64)
     send_to_rows(0)
-    build_kicks()
+    build_kicks(10, 16)
     wait_rows(0)
     kick_rows(0)
     send_to_lines(1)
@@ -308,14 +307,11 @@
     wait_rows(2)
     stage[...] = rows[2].reshape(PARTS * XB, 128).astype(F32)
 
-    def unpack(x, carry):
+    for x in range(XB):
         current = stage[pl.ds(x, 128, stride=XB), :].astype(BF16)
-        turned = nt_dot(eye, current)
+        turned = nt_dot(eye, current).astype(BF16)
         for j in range(4):
             out[x, :, 128 * j : 128 * j + 128] = turned[32 * j : 32 * j + 32, :]
-        return carry
-
-    lax.fori_loop(0, XB, unpack, 0)
     wait_sent(4)
     wait_sent(5)
 
@@ -323,9 +319,9 @@
 def on_device(density, kernel, electrode, drift_sign):
     vmem = pl.BlockSpec(memory_space=pltpu.VMEM)
     smem = pl.BlockSpec(memory_space=pltpu.SMEM)
-    return pl.pallas_call(
+    final = pl.pallas_call(
         whole_kernel,
-        out_shape=jax.ShapeDtypeStruct(density.shape, F32),
+        out_shape=jax.ShapeDtypeStruct(density.shape, BF16),
         in_specs=[vmem, vmem, smem, smem, vmem],
         out_specs=vmem,
         scratch_shapes=[
@@ -337,7 +333,7 @@
             pltpu.VMEM((NX, NX), BF16),
             pltpu.VMEM((NX, NX), BF16),
             pltpu.VMEM((512, 512), BF16),
-            pltpu.VMEM((NP, NP), BF16),
+            pltpu.VMEM((PARTS * XB, 128), F32),
             pltpu.VMEM((XB, NP, NP), BF16),
             pltpu.VMEM((NV, 1, 1024), F32),
             pltpu.SemaphoreType.DMA((6,)),
@@ -347,6 +343,7 @@
             collective_id=0, has_side_effects=True, vmem_limit_bytes=56 << 20
         ),
     )(density, kernel, electrode, drift_sign, jnp.asarray(shift_kernels()))
+    return final.astype(F32)
 
 
 def solution(mesh):

time: 98.9 us -> 83.6 us (0.85)
  Pallas kernels: 95.4 us -> 80.2 us
  local copies, waits for them, and re-layouts: 2.29 us -> 0 us
  other arithmetic: 0 us -> 2.14 us
    pallas_call x1, Pallas kernels: 95.4 us -> 80.2 us  [on_device(): pl.pallas_call(whole_kernel, out_shape=jax.ShapeDtypeStruct(density.shape...]
    unnamed x1 -> x0, local copies, waits for them, and re-layouts: 2.29 us -> none
    convert_element_type x0 -> x1, other arithmetic: none -> 2.14 us  [on_device(): return final.astype(F32)]
where the time goes in v1:
time: 83.6 us; the launch traced here: 82.4 us
  Pallas kernels  80.2 us (96%)
  other arithmetic  2.14 us (3%)
    pallas_call x1, Pallas kernels, on_device(): pl.pallas_call(whole_kernel, out_shape=jax.ShapeDtypeStruct(density.shape...  80.2 us
    convert_element_type x1, other arithmetic, on_device(): return final.astype(F32)  2.14 us

profile of v1, /device:TPU:0, one launch (start us, length us, event | category | flops | bytes accessed | tf_op | source)
XLA Modules:
  0.0 82.4 jit_solution(10169968184575678193)
XLA Ops:
  0.0 80.2 %shard_map.55 = bf16[16,32,512]{2,1,0:T(8,128)(2,1)} custom-call(f32[16,32,512]{2,1,0:T(8,128)} %density.1, bf16[16,512]{1,0:T(8,128)(2,1)} %kernel.1, s32[16]{0:T(128)} %electrode.1, s32[8]{0:T(128)} %drift_sign.1, f32[8,512]{1,0:T(8,128)} %constant.2.clone.taps), custom_call_target="tpu_custom_call" | custom-call | tf_op jit(solution)/shard_map/pallas_call | solution.py:322
  80.2 2.1 %convert_element_type.3 = f32[16,32,512]{2,1,0:T(8,128)} convert(bf16[16,32,512]{2,1,0:T(8,128)(2,1)} %shard_map.55) | non-fusion elementwise | flops 262144 | bytes 1572864 | tf_op jit(solution)/shard_map/convert_element_type | solution.py:346

commit v2 on v1

--- a/solution.py
+++ b/solution.py
@@ -40,45 +40,29 @@
 
 def send_order():
     ring = lambda t: min(t, 4 - t)
-    offsets = [o for o in range(64)]
-    key = lambda o: -(ring(o // 16) + ring(o // 4 % 4) + ring(o % 4))
-    offsets.sort(key=lambda o: (key(o), (o * 37) % 64))
-    offsets = offsets[:63]
-    packed = []
-    for i in range(0, 63, 3):
-        trio = offsets[i : i + 3]
-        packed.append(trio[0] + 64 * trio[1] + 4096 * trio[2])
-    return packed
+    far = lambda o: ring(o // 16) + ring(o // 4 % 4) + ring(o % 4)
+    return sorted(range(1, 64), key=lambda o: (-far(o), (o * 37) % 64))
 
 
 ORDER = send_order()
 
 
-def for_each_peer(me, visit):
+def peers(me):
     y, z, x, core = me
-
-    def group(g, carry):
-        code = jnp.int32(0)
-        for i, value in enumerate(ORDER):
-            code = jnp.where(g == i, jnp.int32(value), code)
-
-        def one(_, code):
-            o = lax.rem(code, 64)
-            y2 = lax.rem(y + o // 16, 4)
-            z2 = lax.rem(z + lax.rem(o // 4, 4), 4)
-            x2 = lax.rem(x + lax.rem(o, 4), 4)
-            gx = y2 * 8 + (x2 // 2) * 4 + z2
-            gy = lax.rem(x2, 2) * 2
-            visit(gx, gy)
-            visit(gx, gy + 1)
-            return code // 64
-
-        lax.fori_loop(0, 3, one, code)
-        return carry
-
-    lax.fori_loop(0, len(ORDER), group, 0)
-    gx = y * 8 + (x // 2) * 4 + z
-    visit(gx, lax.rem(x, 2) * 2 + 1 - core)
+    ys = [lax.rem(y + i, 4) * 8 for i in range(4)]
+    zs = [lax.rem(z + i, 4) for i in range(4)]
+    xs = [lax.rem(x + i, 4) for i in range(4)]
+    high = [t // 2 * 4 for t in xs]
+    low = [lax.rem(t, 2) * 2 for t in xs]
+    everyone, column = [], []
+    for o in ORDER:
+        gx = ys[o // 16] + zs[o // 4 % 4] + high[o % 4]
+        gy = low[o % 4]
+        everyone += [(gx, gy), (gx, gy + 1)]
+        if o % 2 == 0:
+            column.append(gx)
+    everyone.append((ys[0] + zs[0] + high[0], low[0] + 1 - core))
+    return everyone, column
 
 
 def iota(shape, axis):
@@ -105,8 +89,12 @@
     to_rows,
     rows,
     stage,
+    last_lines,
+    last_out,
+    last_rows,
     half,
     double,
+    last,
     drift,
     kicked,
     kick,
@@ -119,18 +107,17 @@
     d = gx * 4 + gy
     me = (gx // 8, lax.rem(gx, 4), lax.rem(gx // 4, 2) * 2 + gy // 2, lax.rem(gy, 2))
 
+    everyone, same_gy = peers(me)
+
     barrier = pltpu.get_barrier_semaphore()
-
-    def greet(a, b):
-        pl.semaphore_signal(barrier, inc=1, device_id=(a, b), device_id_type=MESH)
-
-    for_each_peer(me, greet)
+    for peer in everyone:
+        pl.semaphore_signal(barrier, inc=1, device_id=peer, device_id_type=MESH)
 
     def row_tile(ref, a, b):
         return ref.at[pl.ds(pl.multiple_of(a * XB, XB), XB), pl.ds(pl.multiple_of(b * 128, 128), 128)]
 
     def send_to_lines(r):
-        def push(a, b):
+        for a, b in everyone:
             pltpu.make_async_remote_copy(
                 src_ref=to_lines.at[a * 4 + b],
                 dst_ref=row_tile(lines.at[r], gx, gy),
@@ -139,12 +126,10 @@
                 device_id=(a, b),
                 device_id_type=MESH,
             ).start()
-
-        for_each_peer(me, push)
         pltpu.make_async_copy(to_lines.at[d], row_tile(lines.at[r], gx, gy), recv.at[2 * r]).start()
 
     def send_to_rows(r):
-        def push(a, b):
+        for a, b in everyone:
             pltpu.make_async_remote_copy(
                 src_ref=row_tile(to_rows, a, b),
                 dst_ref=rows.at[r, d],
@@ -153,9 +138,39 @@
                 device_id=(a, b),
                 device_id_type=MESH,
             ).start()
-
-        for_each_peer(me, push)
         pltpu.make_async_copy(row_tile(to_rows, gx, gy), rows.at[r, d], recv.at[2 * r + 1]).start()
+
+    def slab(ref, a):
+        return ref.at[:, pl.ds(pl.multiple_of(a * XB, XB), XB), :]
+
+    def fan(ref, a):
+        return ref.at[:, a]
+
+    def send_last_lines():
+        source = to_lines.reshape(4, 32, XB, 128)
+        for a in same_gy:
+            pltpu.make_async_remote_copy(
+                src_ref=fan(source, a),
+                dst_ref=slab(last_lines, gx),
+                send_sem=send.at[4],
+                recv_sem=recv.at[4],
+                device_id=(a, gy),
+                device_id_type=MESH,
+            ).start()
+        pltpu.make_async_copy(fan(source, gx), slab(last_lines, gx), recv.at[4]).start()
+
+    def send_last_rows():
+        target = last_rows.reshape(4, 32, XB, 128)
+        for a in same_gy:
+            pltpu.make_async_remote_copy(
+                src_ref=slab(last_out, a),
+                dst_ref=fan(target, gx),
+                send_sem=send.at[5],
+                recv_sem=recv.at[5],
+                device_id=(a, gy),
+                device_id_type=MESH,
+            ).start()
+        pltpu.make_async_copy(slab(last_out, gx), fan(target, gx), recv.at[5]).start()
 
     def wait_lines(r):
         pltpu.make_async_copy(lines.at[r], lines.at[r], recv.at[2 * r]).wait()
@@ -163,8 +178,8 @@
     def wait_rows(r):
         pltpu.make_async_copy(rows.at[r], rows.at[r], recv.at[2 * r + 1]).wait()
 
-    def wait_sent(s):
-        sent = to_lines.at[pl.ds(0, PARTS - 1)]
+    def wait_sent(s, tiles=PARTS - 1):
+        sent = to_lines.at[pl.ds(0, tiles)]
         pltpu.make_async_copy(sent, sent, send.at[s]).wait()
 
     eye = (iota((128, 128), 0) == iota((128, 128), 1)).astype(BF16)
@@ -206,14 +221,16 @@
 
     parity = lax.rem(d, 2)
 
-    def circulant(row_even, row_odd, shift):
-        row = jnp.where(parity == 0, row_even, row_odd)
+    def circulant(odd, row_even, row_odd, shift):
+        row = jnp.where(odd == 0, row_even, row_odd)
         row = pltpu.roll(jnp.broadcast_to(row, (8, NX)), shift, 1)[0:1, :]
         wide = jnp.broadcast_to(row, (NX, NX))
         return pltpu.roll(wide, 0, 1, stride=1, stride_axis=0)
 
-    half[...] = circulant(taps[0:1, :], taps[1:2, :], NX - 127 + d // 2).astype(BF16)
-    double[...] = circulant(taps[2:3, :], taps[3:4, :], NX - 255 + d).astype(BF16)
+    half[...] = circulant(parity, taps[0:1, :], taps[1:2, :], NX - 127 + d // 2).astype(BF16)
+    double[...] = circulant(parity, taps[2:3, :], taps[3:4, :], NX - 255 + d).astype(BF16)
+
+    last[...] = circulant(lax.rem(gx, 2), taps[0:1, :], taps[1:2, :], NX - 127 + gx // 2).astype(BF16)
 
     col = iota((16, 512), 1)
     col_y = (col // 128) * 32 + lax.rem(col, 32)
@@ -255,17 +272,25 @@
     lane_block = iota((128, 128), 1) // 32
     wide_block = lax.rem(iota((512, 512), 1) // 32, 4)
 
-    def advect(r, matrix, with_drift, cells):
-        if with_drift:
-            current = dot(lines[r], drift[...]).astype(BF16)
-        else:
-            current = lines[r]
+    def turn(current, block, cells):
         turned = current
-        for j in range(1, 4):
-            cut = cells * j
-            moved = jnp.concatenate([current[cut:], current[:cut]], axis=0)
-            turned = jnp.where(wide_block == j, moved, turned)
+        for j in range(4):
+            cut = cells(j)
+            moved = jnp.concatenate([current[cut:], current[:cut]], axis=0) if cut else current
+            turned = jnp.where(block == j, moved, turned)
+        return turned
+
+    def advect(r, matrix, cells):
+        current = dot(lines[r], drift[...]).astype(BF16)
+        turned = turn(current, wide_block, lambda j: cells * j)
         to_rows[...] = dot(matrix[...], turned).astype(BF16)
+
+    def advect_last():
+        narrow = wide_block[:, :128]
+        turned = [turn(last_lines[h], narrow, lambda j: 64 * j + 16 * h) for h in range(4)]
+        result = dot(last[...], jnp.concatenate(turned, axis=1)).astype(BF16)
+        for h in range(4):
+            last_out[h] = result[:, 128 * h : 128 * h + 128]
 
     def kick_rows(r):
         stage[...] = rows[r].reshape(PARTS * XB, 128).astype(F32)
@@ -287,7 +312,7 @@
 
     build_kicks(4, 10)
     wait_lines(0)
-    advect(0, half, True, 64)
+    advect(0, half, 64)
     send_to_rows(0)
     build_kicks(10, 16)
     wait_rows(0)
@@ -295,25 +320,24 @@
     send_to_lines(1)
     wait_lines(1)
     wait_sent(1)
-    advect(1, double, True, 128)
+    advect(1, double, 128)
     send_to_rows(1)
     wait_rows(1)
     kick_rows(1)
-    send_to_lines(2)
-    wait_lines(2)
+    send_last_lines()
+    pltpu.make_async_copy(last_lines, last_lines, recv.at[4]).wait()
+    advect_last()
+    send_last_rows()
     wait_sent(3)
-    advect(2, half, False, 64)
-    send_to_rows(2)
-    wait_rows(2)
-    stage[...] = rows[2].reshape(PARTS * XB, 128).astype(F32)
-
+    wait_sent(4, PARTS - 4)
+    pltpu.make_async_copy(last_rows, last_rows, recv.at[5]).wait()
+    stage[...] = last_rows[...].reshape(PARTS * XB, 128).astype(F32)
     for x in range(XB):
         current = stage[pl.ds(x, 128, stride=XB), :].astype(BF16)
         turned = nt_dot(eye, current).astype(BF16)
         for j in range(4):
             out[x, :, 128 * j : 128 * j + 128] = turned[32 * j : 32 * j + 32, :]
-    wait_sent(4)
-    wait_sent(5)
+    wait_sent(5, PARTS - 4)
 
 
 def on_device(density, kernel, electrode, drift_sign):
@@ -326,10 +350,14 @@
         out_specs=vmem,
         scratch_shapes=[
             pltpu.VMEM((PARTS, XB, 128), BF16),
-            pltpu.VMEM((3, NX, 512), BF16),
+            pltpu.VMEM((2, NX, 512), BF16),
             pltpu.VMEM((NX, 512), BF16),
-            pltpu.VMEM((3, PARTS, XB, 128), BF16),
+            pltpu.VMEM((2, PARTS, XB, 128), BF16),
             pltpu.VMEM((PARTS * XB, 128), F32),
+            pltpu.VMEM((4, NX, 128), BF16),
+            pltpu.VMEM((4, NX, 128), BF16),
+            pltpu.VMEM((PARTS, XB, 128), BF16),
+            pltpu.VMEM((NX, NX), BF16),
             pltpu.VMEM((NX, NX), BF16),
             pltpu.VMEM((NX, NX), BF16),
             pltpu.VMEM((512, 512), BF16),

time: 83.6 us -> 76.7 us (0.917); the launches traced: 82.4 us -> 76.5 us
  Pallas kernels: 80.2 us -> 74.3 us
    pallas_call x1, Pallas kernels: 80.2 us -> 74.3 us  [on_device(): pl.pallas_call(whole_kernel, out_shape=jax.ShapeDtypeStruct(density.shape...]
where the time goes in v2:
time: 76.7 us; the launch traced here: 76.5 us
  Pallas kernels  74.3 us (97%)
  other arithmetic  2.14 us (3%)
    pallas_call x1, Pallas kernels, on_device(): pl.pallas_call(whole_kernel, out_shape=jax.ShapeDtypeStruct(density.shape...  74.3 us
    convert_element_type x1, other arithmetic, on_device(): return final.astype(F32)  2.14 us

profile of v2, /device:TPU:0, one launch (start us, length us, event | category | flops | bytes accessed | tf_op | source)
XLA Modules:
  0.0 76.5 jit_solution(17343446550085564223)
XLA Ops:
  0.0 74.3 %shard_map.55 = bf16[16,32,512]{2,1,0:T(8,128)(2,1)} custom-call(f32[16,32,512]{2,1,0:T(8,128)} %density.1, bf16[16,512]{1,0:T(8,128)(2,1)} %kernel.1, s32[16]{0:T(128)} %electrode.1, s32[8]{0:T(128)} %drift_sign.1, f32[8,512]{1,0:T(8,128)} %constant.2.clone.taps), custom_call_target="tpu_custom_call" | custom-call | tf_op jit(solution)/shard_map/pallas_call | solution.py:346
  74.4 2.1 %convert_element_type.3 = f32[16,32,512]{2,1,0:T(8,128)} convert(bf16[16,32,512]{2,1,0:T(8,128)(2,1)} %shard_map.55) | non-fusion elementwise | flops 262144 | bytes 1572864 | tf_op jit(solution)/shard_map/convert_element_type | solution.py:374

commit v3 on v2

--- a/solution.py
+++ b/solution.py
@@ -49,20 +49,29 @@
 
 def peers(me):
     y, z, x, core = me
-    ys = [lax.rem(y + i, 4) * 8 for i in range(4)]
+    across = lax.rem(y + 2, 4)
+    mate = lambda t: t + 1 - 2 * lax.rem(t, 2)
+    ys = [8 * t for t in (y, mate(across), across, mate(y))]
     zs = [lax.rem(z + i, 4) for i in range(4)]
     xs = [lax.rem(x + i, 4) for i in range(4)]
     high = [t // 2 * 4 for t in xs]
     low = [lax.rem(t, 2) * 2 for t in xs]
     everyone, column = [], []
+    parts = ([], []), ([], [])
     for o in ORDER:
         gx = ys[o // 16] + zs[o // 4 % 4] + high[o % 4]
         gy = low[o % 4]
-        everyone += [(gx, gy), (gx, gy + 1)]
+        part, part_column = parts[0 if o // 16 in (1, 2) else 1]
+        pair = [(gx, gy), (gx, gy + 1)]
+        everyone += pair
+        part += pair
         if o % 2 == 0:
             column.append(gx)
-    everyone.append((ys[0] + zs[0] + high[0], low[0] + 1 - core))
-    return everyone, column
+            part_column.append(gx)
+    sibling = (ys[0] + zs[0] + high[0], low[0] + 1 - core)
+    everyone.append(sibling)
+    parts[1][0].append(sibling)
+    return everyone, column, parts
 
 
 def iota(shape, axis):
@@ -97,6 +106,7 @@
     last,
     drift,
     kicked,
+    operands,
     kick,
     offsets,
     send,
@@ -107,7 +117,9 @@
     d = gx * 4 + gy
     me = (gx // 8, lax.rem(gx, 4), lax.rem(gx // 4, 2) * 2 + gy // 2, lax.rem(gy, 2))
 
-    everyone, same_gy = peers(me)
+    everyone, same_gy, ((far, far_gy), (near, near_gy)) = peers(me)
+    near_pair = me[0] // 2
+    far_pair = 1 - near_pair
 
     barrier = pltpu.get_barrier_semaphore()
     for peer in everyone:
@@ -116,8 +128,8 @@
     def row_tile(ref, a, b):
         return ref.at[pl.ds(pl.multiple_of(a * XB, XB), XB), pl.ds(pl.multiple_of(b * 128, 128), 128)]
 
-    def send_to_lines(r):
-        for a, b in everyone:
+    def send_to_lines(r, group):
+        for a, b in group:
             pltpu.make_async_remote_copy(
                 src_ref=to_lines.at[a * 4 + b],
                 dst_ref=row_tile(lines.at[r], gx, gy),
@@ -126,10 +138,12 @@
                 device_id=(a, b),
                 device_id_type=MESH,
             ).start()
+
+    def keep_lines(r):
         pltpu.make_async_copy(to_lines.at[d], row_tile(lines.at[r], gx, gy), recv.at[2 * r]).start()
 
-    def send_to_rows(r):
-        for a, b in everyone:
+    def send_to_rows(r, group):
+        for a, b in group:
             pltpu.make_async_remote_copy(
                 src_ref=row_tile(to_rows, a, b),
                 dst_ref=rows.at[r, d],
@@ -138,6 +152,8 @@
                 device_id=(a, b),
                 device_id_type=MESH,
             ).start()
+
+    def keep_rows(r):
         pltpu.make_async_copy(row_tile(to_rows, gx, gy), rows.at[r, d], recv.at[2 * r + 1]).start()
 
     def slab(ref, a):
@@ -146,9 +162,9 @@
     def fan(ref, a):
         return ref.at[:, a]
 
-    def send_last_lines():
+    def send_last_lines(group):
         source = to_lines.reshape(4, 32, XB, 128)
-        for a in same_gy:
+        for a in group:
             pltpu.make_async_remote_copy(
                 src_ref=fan(source, a),
                 dst_ref=slab(last_lines, gx),
@@ -157,11 +173,14 @@
                 device_id=(a, gy),
                 device_id_type=MESH,
             ).start()
+
+    def keep_last_lines():
+        source = to_lines.reshape(4, 32, XB, 128)
         pltpu.make_async_copy(fan(source, gx), slab(last_lines, gx), recv.at[4]).start()
 
-    def send_last_rows():
+    def send_last_rows(group):
         target = last_rows.reshape(4, 32, XB, 128)
-        for a in same_gy:
+        for a in group:
             pltpu.make_async_remote_copy(
                 src_ref=slab(last_out, a),
                 dst_ref=fan(target, gx),
@@ -170,6 +189,9 @@
                 device_id=(a, gy),
                 device_id_type=MESH,
             ).start()
+
+    def keep_last_rows():
+        target = last_rows.reshape(4, 32, XB, 128)
         pltpu.make_async_copy(slab(last_out, gx), fan(target, gx), recv.at[5]).start()
 
     def wait_lines(r):
@@ -217,7 +239,8 @@
 
     build_kicks(0, 4)
     pl.semaphore_wait(barrier, PARTS - 1)
-    send_to_lines(0)
+    send_to_lines(0, everyone)
+    keep_lines(0)
 
     parity = lax.rem(d, 2)
 
@@ -283,51 +306,91 @@
     def advect(r, matrix, cells):
         current = dot(lines[r], drift[...]).astype(BF16)
         turned = turn(current, wide_block, lambda j: cells * j)
-        to_rows[...] = dot(matrix[...], turned).astype(BF16)
+        for pair, group in ((far_pair, far), (near_pair, near)):
+            at = pl.ds(pl.multiple_of(256 * pair, 256), 256)
+            to_rows[at, :] = dot(matrix[at, :], turned).astype(BF16)
+            send_to_rows(r, group)
+        keep_rows(r)
 
     def advect_last():
         narrow = wide_block[:, :128]
         turned = [turn(last_lines[h], narrow, lambda j: 64 * j + 16 * h) for h in range(4)]
-        result = dot(last[...], jnp.concatenate(turned, axis=1)).astype(BF16)
-        for h in range(4):
-            last_out[h] = result[:, 128 * h : 128 * h + 128]
-
-    def kick_rows(r):
+        turned = jnp.concatenate(turned, axis=1)
+        for pair, group in ((far_pair, far_gy), (near_pair, near_gy)):
+            at = pl.ds(pl.multiple_of(256 * pair, 256), 256)
+            result = dot(last[at, :], turned).astype(BF16)
+            for h in range(4):
+                last_out[h, at, :] = result[:, 128 * h : 128 * h + 128]
+            send_last_rows(group)
+        keep_last_rows()
+
+    def kick_rows(r, pieces, sends, send_group, keep):
         stage[...] = rows[r].reshape(PARTS * XB, 128).astype(F32)
-        for start in range(0, XB, 4):
-            group = range(start, start + 4)
-            current = [stage[pl.ds(x, 128, stride=XB), :] for x in group]
-            operand = [
-                jnp.concatenate([c] + [pltpu.roll(c, 32 * k, 1) for k in range(1, 4)], axis=0).astype(BF16)
-                for c in current
-            ]
-            product = [dot(kick[x], o) for x, o in zip(group, operand)]
-            for x, c, q in zip(group, current, product):
-                change = q[0:128]
-                for j in range(1, 4):
-                    change = jnp.where(lane_block == j, q[128 * j : 128 * j + 128], change)
-                kicked[pl.ds(x, 128, stride=XB), :] = c + change
         wait_sent(2 * r)
-        to_lines[...] = kicked[...].astype(BF16).reshape(PARTS, XB, 128)
+        for part, pair in enumerate((far_pair, near_pair)):
+            if part == 1:
+                send_group(sends[0])
+            runs = pieces(pair)
+            total = sum(count for _, count in runs)
+            for start in range(0, XB, 4):
+                group = range(start, start + 4)
+                if part == 0:
+                    current = [stage[pl.ds(x, 128, stride=XB), :] for x in group]
+                    for x, c in zip(group, current):
+                        operands[x] = jnp.concatenate(
+                            [c] + [pltpu.roll(c, 32 * k, 1) for k in range(1, 4)], axis=0
+                        ).astype(BF16)
+                product = []
+                for x in group:
+                    left = jnp.concatenate(
+                        [
+                            kick[x, pl.ds(pl.multiple_of(128 * j + first, 16), count), :]
+                            for j in range(4)
+                            for first, count in runs
+                        ],
+                        axis=0,
+                    )
+                    product.append(dot(left, operands[x]))
+                for x, q in zip(group, product):
+                    change = q[0:total]
+                    for j in range(1, 4):
+                        change = jnp.where(lane_block[0:total] == j, q[total * j : total * j + total], change)
+                    done = 0
+                    for first, count in runs:
+                        at = pl.ds(XB * first + x, count, stride=XB)
+                        kicked[at, :] = stage[at, :] + change[done : done + count]
+                        done += count
+            for first, count in runs:
+                block = kicked[pl.ds(pl.multiple_of(XB * first, 256), XB * count), :]
+                to_lines[pl.ds(first, count)] = block.astype(BF16).reshape(count, XB, 128)
+        send_group(sends[1])
+        keep()
 
     build_kicks(4, 10)
     wait_lines(0)
     advect(0, half, 64)
-    send_to_rows(0)
     build_kicks(10, 16)
     wait_rows(0)
-    kick_rows(0)
-    send_to_lines(1)
+    kick_rows(
+        0,
+        lambda pair: [(64 * pair, 64)],
+        (far, near),
+        lambda group: send_to_lines(1, group),
+        lambda: keep_lines(1),
+    )
     wait_lines(1)
     wait_sent(1)
     advect(1, double, 128)
-    send_to_rows(1)
     wait_rows(1)
-    kick_rows(1)
-    send_last_lines()
+    kick_rows(
+        1,
+        lambda pair: [(32 * h + 16 * pair, 16) for h in range(4)],
+        (far_gy, near_gy),
+        send_last_lines,
+        keep_last_lines,
+    )
     pltpu.make_async_copy(last_lines, last_lines, recv.at[4]).wait()
     advect_last()
-    send_last_rows()
     wait_sent(3)
     wait_sent(4, PARTS - 4)
     pltpu.make_async_copy(last_rows, last_rows, recv.at[5]).wait()
@@ -362,6 +425,7 @@
             pltpu.VMEM((NX, NX), BF16),
             pltpu.VMEM((512, 512), BF16),
             pltpu.VMEM((PARTS * XB, 128), F32),
+            pltpu.VMEM((XB, NP, 128), BF16),
             pltpu.VMEM((XB, NP, NP), BF16),
             pltpu.VMEM((NV, 1, 1024), F32),
             pltpu.SemaphoreType.DMA((6,)),

time: 76.7 us -> 74.8 us (0.975)
  Pallas kernels: 74.3 us -> 72.1 us
    pallas_call x1, Pallas kernels: 74.3 us -> 72.1 us  [on_device(): pl.pallas_call(whole_kernel, out_shape=jax.ShapeDtypeStruct(density.shape...]
where the time goes in v3:
time: 74.8 us; the launch traced here: 74.3 us
  Pallas kernels  72.1 us (96%)
  other arithmetic  2.14 us (3%)
    pallas_call x1, Pallas kernels, on_device(): pl.pallas_call(whole_kernel, out_shape=jax.ShapeDtypeStruct(density.shape...  72.1 us
    convert_element_type x1, other arithmetic, on_device(): return final.astype(F32)  2.14 us

profile of v3, /device:TPU:0, one launch (start us, length us, event | category | flops | bytes accessed | tf_op | source)
XLA Modules:
  0.0 74.3 jit_solution(17754060051370757732)
XLA Ops:
  0.0 72.1 %shard_map.55 = bf16[16,32,512]{2,1,0:T(8,128)(2,1)} custom-call(f32[16,32,512]{2,1,0:T(8,128)} %density.1, bf16[16,512]{1,0:T(8,128)(2,1)} %kernel.1, s32[16]{0:T(128)} %electrode.1, s32[8]{0:T(128)} %drift_sign.1, f32[8,512]{1,0:T(8,128)} %constant.2.clone.taps), custom_call_target="tpu_custom_call" | custom-call | tf_op jit(solution)/shard_map/pallas_call | solution.py:409
  72.1 2.1 %convert_element_type.3 = f32[16,32,512]{2,1,0:T(8,128)} convert(bf16[16,32,512]{2,1,0:T(8,128)(2,1)} %shard_map.55) | non-fusion elementwise | flops 262144 | bytes 1572864 | tf_op jit(solution)/shard_map/convert_element_type | solution.py:438

commit v4 on v3

--- a/solution.py
+++ b/solution.py
@@ -41,7 +41,7 @@
 def send_order():
     ring = lambda t: min(t, 4 - t)
     far = lambda o: ring(o // 16) + ring(o // 4 % 4) + ring(o % 4)
-    return sorted(range(1, 64), key=lambda o: (-far(o), (o * 37) % 64))
+    return sorted(range(1, 64), key=lambda o: (-far(o), (o * 11) % 64))
 
 
 ORDER = send_order()
@@ -332,8 +332,8 @@
                 send_group(sends[0])
             runs = pieces(pair)
             total = sum(count for _, count in runs)
-            for start in range(0, XB, 4):
-                group = range(start, start + 4)
+            for start in range(0, XB, 8):
+                group = range(start, start + 8)
                 if part == 0:
                     current = [stage[pl.ds(x, 128, stride=XB), :] for x in group]
                     for x, c in zip(group, current):

time: 74.8 us -> 74.5 us (level)
  no operation moved by 1% of the time
where the time goes in v4:
time: 74.5 us; the launch traced here: 74.3 us
  Pallas kernels  72.1 us (97%)
  other arithmetic  2.14 us (3%)
    pallas_call x1, Pallas kernels, on_device(): pl.pallas_call(whole_kernel, out_shape=jax.ShapeDtypeStruct(density.shape...  72.1 us
    convert_element_type x1, other arithmetic, on_device(): return final.astype(F32)  2.14 us

profile of v4, /device:TPU:0, one launch (start us, length us, event | category | flops | bytes accessed | tf_op | source)
XLA Modules:
  0.0 74.3 jit_solution(14684939124498866829)
XLA Ops:
  0.0 72.1 %shard_map.55 = bf16[16,32,512]{2,1,0:T(8,128)(2,1)} custom-call(f32[16,32,512]{2,1,0:T(8,128)} %density.1, bf16[16,512]{1,0:T(8,128)(2,1)} %kernel.1, s32[16]{0:T(128)} %electrode.1, s32[8]{0:T(128)} %drift_sign.1, f32[8,512]{1,0:T(8,128)} %constant.2.clone.taps), custom_call_target="tpu_custom_call" | custom-call | tf_op jit(solution)/shard_map/pallas_call | solution.py:409
  72.1 2.1 %convert_element_type.3 = f32[16,32,512]{2,1,0:T(8,128)} convert(bf16[16,32,512]{2,1,0:T(8,128)(2,1)} %shard_map.55) | non-fusion elementwise | flops 262144 | bytes 1572864 | tf_op jit(solution)/shard_map/convert_element_type | solution.py:438

commit v5 on v4

--- a/solution.py
+++ b/solution.py
@@ -209,7 +209,7 @@
     for x in range(XB):
         block = jnp.concatenate([density[x, :, 128 * j : 128 * j + 128] for j in range(4)], axis=0)
         stage[pl.ds(x, 128, stride=XB), :] = nt_dot(eye, block.astype(BF16))
-    to_lines[...] = stage[...].astype(BF16).reshape(PARTS, XB, 128)
+    to_lines[...] = stage[0 : PARTS * XB, :].astype(BF16).reshape(PARTS, XB, 128)
 
     flip = (iota((512, 512), 0) == lax.rem(512 - iota((512, 512), 1), 512)).astype(BF16)
     forward = kernel[...].astype(F32)
@@ -325,7 +325,7 @@
         keep_last_rows()
 
     def kick_rows(r, pieces, sends, send_group, keep):
-        stage[...] = rows[r].reshape(PARTS * XB, 128).astype(F32)
+        stage[0 : PARTS * XB, :] = rows[r].reshape(PARTS * XB, 128).astype(F32)
         wait_sent(2 * r)
         for part, pair in enumerate((far_pair, near_pair)):
             if part == 1:
@@ -394,7 +394,7 @@
     wait_sent(3)
     wait_sent(4, PARTS - 4)
     pltpu.make_async_copy(last_rows, last_rows, recv.at[5]).wait()
-    stage[...] = last_rows[...].reshape(PARTS * XB, 128).astype(F32)
+    stage[0 : PARTS * XB, :] = last_rows[...].reshape(PARTS * XB, 128).astype(F32)
     for x in range(XB):
         current = stage[pl.ds(x, 128, stride=XB), :].astype(BF16)
         turned = nt_dot(eye, current).astype(BF16)
@@ -416,7 +416,7 @@
             pltpu.VMEM((2, NX, 512), BF16),
             pltpu.VMEM((NX, 512), BF16),
             pltpu.VMEM((2, PARTS, XB, 128), BF16),
-            pltpu.VMEM((PARTS * XB, 128), F32),
+            pltpu.VMEM((PARTS * XB + XB, 128), F32),
             pltpu.VMEM((4, NX, 128), BF16),
             pltpu.VMEM((4, NX, 128), BF16),
             pltpu.VMEM((PARTS, XB, 128), BF16),
@@ -424,7 +424,7 @@
             pltpu.VMEM((NX, NX), BF16),
             pltpu.VMEM((NX, NX), BF16),
             pltpu.VMEM((512, 512), BF16),
-            pltpu.VMEM((PARTS * XB, 128), F32),
+            pltpu.VMEM((PARTS * XB + XB, 128), F32),
             pltpu.VMEM((XB, NP, 128), BF16),
             pltpu.VMEM((XB, NP, NP), BF16),
             pltpu.VMEM((NV, 1, 1024), F32),

time: 74.5 us -> 74.6 us (level)
  no operation moved by 1% of the time
where the time goes in v5:
time: 74.6 us; the launch traced here: 74.4 us
  Pallas kernels  72.2 us (97%)
  other arithmetic  2.14 us (3%)
    pallas_call x1, Pallas kernels, on_device(): pl.pallas_call(whole_kernel, out_shape=jax.ShapeDtypeStruct(density.shape...  72.2 us
    convert_element_type x1, other arithmetic, on_device(): return final.astype(F32)  2.14 us

profile of v5, /device:TPU:0, one launch (start us, length us, event | category | flops | bytes accessed | tf_op | source)
XLA Modules:
  0.0 74.4 jit_solution(11635611789185984101)
XLA Ops:
  0.0 72.2 %shard_map.55 = bf16[16,32,512]{2,1,0:T(8,128)(2,1)} custom-call(f32[16,32,512]{2,1,0:T(8,128)} %density.1, bf16[16,512]{1,0:T(8,128)(2,1)} %kernel.1, s32[16]{0:T(128)} %electrode.1, s32[8]{0:T(128)} %drift_sign.1, f32[8,512]{1,0:T(8,128)} %constant.2.clone.taps), custom_call_target="tpu_custom_call" | custom-call | tf_op jit(solution)/shard_map/pallas_call | solution.py:409
  72.2 2.1 %convert_element_type.3 = f32[16,32,512]{2,1,0:T(8,128)} convert(bf16[16,32,512]{2,1,0:T(8,128)(2,1)} %shard_map.55) | non-fusion elementwise | flops 262144 | bytes 1572864 | tf_op jit(solution)/shard_map/convert_element_type | solution.py:438
